TPU v7x, 128 devices: a whole 4x4x4 slice. The times are simulated.
128 devices in a mesh: shot: 4 (over y_lo, core), gx: 4 (over z), gy: 8 (over x, y_hi).
Axes of the slice: x: 4, y: 4 (y_hi: 2, y_lo: 2; y = y_hi * 2 + y_lo), z: 4, core: 2. Of those that a mesh axis runs over, the one named last changes fastest.
Arguments:
- model_tiles: float32 [256, 256, 128], P(('shot', 'gx'), 'gy'), may hold values from 0.2 to 0.45
- owner_map: int32 [16], replicated, may hold values from 0 to 15, each once
- offsets: int32 [4], P('shot'), may hold values from 0 to 12
- field_now: float32 [4, 2, 64, 256, 128], P('shot', None, 'gx', 'gy'), may hold values from -6 to 6
- field_prev: float32 [4, 2, 64, 256, 128], P('shot', None, 'gx', 'gy'), may hold values from -6 to 6
- sources: int32 [4, 2, 3], P('shot'), may hold values from 0 to 255, as said below
- wavelet: float32 [4, 2, 8], P('shot'), may hold values from -6 to 6
- receivers: int32 [4, 256, 3], P('shot'), may hold values from 0 to 255, as said below
Outputs:
- out_now: float32 [4, 2, 64, 256, 128], P('shot', None, 'gx', 'gy')
- out_prev: float32 [4, 2, 64, 256, 128], P('shot', None, 'gx', 'gy')
- traces: float32 [4, 2, 256, 8], P('shot')
Inputs may be any that keep to these rules, and one draw needn't show every extreme that they name: `sources`: each row is a cell of the group's aperture: first entry below 64, second below 256, third below 128. `receivers`: each row is a cell of the group's aperture: first entry below 64, second below 256, third below 128.
All inputs are finite; a program needn't handle non-finite values.
Results may differ from a plain program's by a relative error of at most 0.0003.
Values sent between devices are 32-bit elements; how exact they have to be, the bound alone decides.
A program may use at most 128 MiB of HBM per device.

v0:
```python
import jax
import jax.numpy as jnp
from jax import lax
from jax.sharding import PartitionSpec as P

STEPS = 8
center_weight = -2.5
near_weight = 4.0 / 3.0
far_weight = -1.0 / 12.0
damp_peak = 0.3


def extended_2(cells, sides, width):
    for axis, dim in sides:
        count = lax.axis_size(axis)
        ends = count - 1
        head = lax.slice_in_dim(cells, 0, width, axis=dim)
        tail = lax.slice_in_dim(cells, cells.shape[dim] - width, cells.shape[dim], axis=dim)
        cells = jnp.concatenate(
            [
                lax.ppermute(tail, axis, [(i, (i + 1) % count) for i in range(ends)]),
                cells,
                lax.ppermute(head, axis, [((i + 1) % count, i) for i in range(ends)]),
            ],
            axis=dim,
        )
    return cells


def depth_ahead(field, reach):
    filler = jnp.zeros(field.shape[:-1] + (reach,), field.dtype)
    return jnp.concatenate([field[..., reach:], filler], axis=-1)


def depth_behind(field, reach):
    filler = jnp.zeros(field.shape[:-1] + (reach,), field.dtype)
    return jnp.concatenate([filler, field[..., :-reach]], axis=-1)


def laplace(extended):
    middle = extended[:, 2:-2, 2:-2]
    along_x = (
        center_weight * middle
        + near_weight * (extended[:, 3:-1, 2:-2] + extended[:, 1:-3, 2:-2])
        + far_weight * (extended[:, 4:, 2:-2] + extended[:, :-4, 2:-2])
    )
    along_y = (
        center_weight * middle
        + near_weight * (extended[:, 2:-2, 3:-1] + extended[:, 2:-2, 1:-3])
        + far_weight * (extended[:, 2:-2, 4:] + extended[:, 2:-2, :-4])
    )
    along_z = (
        center_weight * middle
        + near_weight * (depth_ahead(middle, 1) + depth_behind(middle, 1))
        + far_weight * (depth_ahead(middle, 2) + depth_behind(middle, 2))
    )
    return along_x + along_y + along_z


def damping(x_cells, y_cells, width, x_total, y_total):
    x_depth = (
        jnp.maximum(width - jnp.minimum(x_cells + 1, x_total - x_cells), 0).astype(jnp.float32)
        / width
    )
    y_depth = (
        jnp.maximum(width - jnp.minimum(y_cells + 1, y_total - y_cells), 0).astype(jnp.float32)
        / width
    )
    return damp_peak * (x_depth[:, None] * x_depth[:, None] + y_depth[None, :] * y_depth[None, :])


def injection(x_cells, y_cells, z_cells, source_cells, amplitude):
    on_x = (x_cells[None, :] == source_cells[:, 0:1]).astype(jnp.float32)
    on_y = (y_cells[None, :] == source_cells[:, 1:2]).astype(jnp.float32)
    on_z = (z_cells[None, :] == source_cells[:, 2:3]).astype(jnp.float32)
    return (
        amplitude[:, None, None, None]
        * on_x[:, :, None, None]
        * on_y[:, None, :, None]
        * on_z[:, None, None, :]
    )


def advance(extended, previous, coef, damp, inject):
    middle = extended[:, 2:-2, 2:-2]
    return (2.0 * middle - (1.0 - damp) * previous + coef * laplace(extended) + inject) / (
        1.0 + damp
    )


def sample(field, receiver_cells, x_start, y_start):
    size_x, size_y = (field.shape[1], field.shape[2])
    local_x = receiver_cells[:, 0] - x_start
    local_y = receiver_cells[:, 1] - y_start
    inside = (local_x >= 0) & (local_x < size_x) & (local_y >= 0) & (local_y < size_y)
    values = field[
        :, jnp.clip(local_x, 0, size_x - 1), jnp.clip(local_y, 0, size_y - 1), receiver_cells[:, 2]
    ]
    return jnp.where(inside[None, :], values, 0.0)


def local(model_tiles, owner_map, offsets, field_now, field_prev, sources, wavelet, receivers):
    block_x, block_y, depth = model_tiles.shape
    column_index = lax.axis_index("gx")
    row_index = lax.axis_index("gy")
    across = lax.axis_size("gx")
    total_x = block_x * across
    total_y = block_y * lax.axis_size("gy")
    shift_x = offsets[0]
    tile_total = owner_map.shape[0]
    column_ids = jnp.arange(tile_total, dtype=jnp.int32)
    wanted = jnp.sum(jnp.where(column_ids == shift_x + column_index, owner_map, 0))
    piece = lax.all_gather(model_tiles, ("shot", "gx"), axis=0, tiled=True)
    rows = wanted * block_x + jnp.arange(block_x, dtype=jnp.int32)
    inside = (rows >= 0) & (rows < piece.shape[0])
    taken = jnp.take(piece, jnp.clip(rows, 0, piece.shape[0] - 1), axis=0)
    speed = jnp.where(inside[:, None, None], taken, jnp.zeros_like(model_tiles))
    coef = speed * speed
    current = field_now[0]
    previous = field_prev[0]
    source_cells = sources[0]
    amplitudes = wavelet[0]
    receiver_cells = receivers[0]
    x_start = column_index * block_x
    y_start = row_index * block_y
    x_here = x_start + jnp.arange(block_x, dtype=jnp.int32)
    y_here = y_start + jnp.arange(block_y, dtype=jnp.int32)
    z_cells = jnp.arange(depth, dtype=jnp.int32)
    damp = damping(x_here, y_here, block_x, total_x, total_y)[:, :, None]
    recorded = []
    for step in range(STEPS):
        extended = extended_2(current, (("gx", 1), ("gy", 2)), 2)
        inject = injection(x_here, y_here, z_cells, source_cells, amplitudes[:, step])
        fresh = advance(extended, previous, coef, damp, inject)
        recorded.append(sample(fresh, receiver_cells, x_start, y_start))
        previous = current
        current = fresh
    traces = lax.psum(jnp.stack(recorded, axis=-1), ("gx", "gy"))
    return (current[None], previous[None], traces[None])


def solution(mesh):
    return jax.shard_map(
        local,
        mesh=mesh,
        in_specs=(
            P(("shot", "gx"), "gy", None),
            P(),
            P("shot"),
            P("shot", None, "gx", "gy", None),
            P("shot", None, "gx", "gy", None),
            P("shot", None, None),
            P("shot", None, None),
            P("shot", None, None),
        ),
        out_specs=(
            P("shot", None, "gx", "gy", None),
            P("shot", None, "gx", "gy", None),
            P("shot", None, None, None),
        ),
        check_vma=False,
    )
```

profile of v0, /device:TPU:0, one launch (start us, length us, event | category | flops | bytes accessed | tf_op | source)
XLA Modules:
  0.0 552.9 jit_solution(16876477504030605119)
XLA Ops:
  28.2 6.1 %collective-permute-start.3 = (f32[2,20,2,128]{3,2,1,0:T(2,128)S(1)}, f32[2,20,2,128]{3,2,1,0:T(2,128)S(1)}, u32[]{:S(2)}, u32[]{:S(2)}) collective-permute-start(f32[2,20,2,128]{3,2,1,0:T(2,128)S(1)} %get-tuple-element.57), channel_id=1, source_target_pairs={{0,1},{1,2},{2,3},{3,4},{4,5},{5,6},{6,7},{8,9},{9,10},{10,11},{11... | collective-permute-start | bytes 122888 | tf_op jit(solution)/shard_map/ppermute | solution.py:21
  37.5 24.6 %all-gather.2.cloned.1.call-done = f32[256,32,128]{2,1,0:T(8,128)} async-done(((f32[16,32,128]{2,1,0:T(8,128)}), f32[256,32,128]{2,1,0:T(8,128)}) %all-gather.2.cloned.1.call-update) | async-done | bytes 4194320 | tf_op jit(solution)/shard_map/all_gather | solution.py:113
  77.4 6.1 %collective-permute-start.7 = (f32[2,20,2,128]{3,2,1,0:T(2,128)S(1)}, f32[2,20,2,128]{3,2,1,0:T(2,128)S(1)}, u32[]{:S(2)}, u32[]{:S(2)}) collective-permute-start(f32[2,20,2,128]{3,2,1,0:T(2,128)S(1)} %get-tuple-element.53), channel_id=1, source_target_pairs={{0,1},{1,2},{2,3},{3,4},{4,5},{5,6},{6,7},{8,9},{9,10},{10,11},{11... | collective-permute-start | bytes 122888 | tf_op jit(solution)/shard_map/ppermute | solution.py:21
  84.4 16.7 %copy.515 = f32[2,16,32,128]{0,3,2,1:T(8,128)} copy(f32[2,16,32,128]{3,2,1,0:T(8,128)S(1)} %fusion.94) | data formatting | bytes 1048576 | tf_op jit(solution)/shard_map/div | solution.py:86
  107.5 5.0 collective-permute-start.9
  115.8 6.5 %collective-permute-start.11 = (f32[2,20,2,128]{3,2,1,0:T(2,128)S(1)}, f32[2,20,2,128]{3,2,1,0:T(2,128)S(1)}, u32[]{:S(2)}, u32[]{:S(2)}) collective-permute-start(f32[2,20,2,128]{3,2,1,0:T(2,128)S(1)} %get-tuple-element.49), channel_id=1, source_target_pairs={{0,1},{1,2},{2,3},{3,4},{4,5},{5,6},{6,7},{8,9},{9,10},{10,11},{11... | collective-permute-start | bytes 122888 | tf_op jit(solution)/shard_map/ppermute | solution.py:21
  123.2 16.7 %copy.516 = f32[2,16,32,128]{0,3,2,1:T(8,128)} copy(f32[2,16,32,128]{3,2,1,0:T(8,128)S(1)} %fusion.82) | data formatting | bytes 1048576 | tf_op jit(solution)/shard_map/div | solution.py:86
  146.4 4.9 collective-permute-start.13
  154.5 6.9 %collective-permute-start.15 = (f32[2,20,2,128]{3,2,1,0:T(2,128)S(1)}, f32[2,20,2,128]{3,2,1,0:T(2,128)S(1)}, u32[]{:S(2)}, u32[]{:S(2)}) collective-permute-start(f32[2,20,2,128]{3,2,1,0:T(2,128)S(1)} %get-tuple-element.45), channel_id=1, source_target_pairs={{0,1},{1,2},{2,3},{3,4},{4,5},{5,6},{6,7},{8,9},{9,10},{10,11},{11... | collective-permute-start | bytes 122888 | tf_op jit(solution)/shard_map/ppermute | solution.py:21
  162.4 16.7 %copy.517 = f32[2,16,32,128]{0,3,2,1:T(8,128)} copy(f32[2,16,32,128]{3,2,1,0:T(8,128)S(1)} %fusion.70) | data formatting | bytes 1048576 | tf_op jit(solution)/shard_map/div | solution.py:86
  185.6 4.9 collective-permute-start.17
  193.7 7.1 %collective-permute-start.19 = (f32[2,20,2,128]{3,2,1,0:T(2,128)S(1)}, f32[2,20,2,128]{3,2,1,0:T(2,128)S(1)}, u32[]{:S(2)}, u32[]{:S(2)}) collective-permute-start(f32[2,20,2,128]{3,2,1,0:T(2,128)S(1)} %get-tuple-element.41), channel_id=1, source_target_pairs={{0,1},{1,2},{2,3},{3,4},{4,5},{5,6},{6,7},{8,9},{9,10},{10,11},{11... | collective-permute-start | bytes 122888 | tf_op jit(solution)/shard_map/ppermute | solution.py:21
  201.7 16.7 %copy.518 = f32[2,16,32,128]{0,3,2,1:T(8,128)} copy(f32[2,16,32,128]{3,2,1,0:T(8,128)S(1)} %fusion.58) | data formatting | bytes 1048576 | tf_op jit(solution)/shard_map/div | solution.py:86
  224.9 4.9 collective-permute-start.21
  233.0 6.9 %collective-permute-start.23 = (f32[2,20,2,128]{3,2,1,0:T(2,128)S(1)}, f32[2,20,2,128]{3,2,1,0:T(2,128)S(1)}, u32[]{:S(2)}, u32[]{:S(2)}) collective-permute-start(f32[2,20,2,128]{3,2,1,0:T(2,128)S(1)} %get-tuple-element.37), channel_id=1, source_target_pairs={{0,1},{1,2},{2,3},{3,4},{4,5},{5,6},{6,7},{8,9},{9,10},{10,11},{11... | collective-permute-start | bytes 122888 | tf_op jit(solution)/shard_map/ppermute | solution.py:21
  240.9 16.7 %copy.519 = f32[2,16,32,128]{0,3,2,1:T(8,128)} copy(f32[2,16,32,128]{3,2,1,0:T(8,128)S(1)} %fusion.46) | data formatting | bytes 1048576 | tf_op jit(solution)/shard_map/div | solution.py:86
  264.1 4.9 collective-permute-start.25
  272.2 6.9 %collective-permute-start.27 = (f32[2,20,2,128]{3,2,1,0:T(2,128)S(1)}, f32[2,20,2,128]{3,2,1,0:T(2,128)S(1)}, u32[]{:S(2)}, u32[]{:S(2)}) collective-permute-start(f32[2,20,2,128]{3,2,1,0:T(2,128)S(1)} %get-tuple-element.33), channel_id=1, source_target_pairs={{0,1},{1,2},{2,3},{3,4},{4,5},{5,6},{6,7},{8,9},{9,10},{10,11},{11... | collective-permute-start | bytes 122888 | tf_op jit(solution)/shard_map/ppermute | solution.py:21
  280.1 16.7 %copy.520 = f32[2,16,32,128]{0,3,2,1:T(8,128)} copy(f32[2,16,32,128]{3,2,1,0:T(8,128)S(1)} %fusion.34) | data formatting | bytes 1048576 | tf_op jit(solution)/shard_map/div | solution.py:86
  303.2 4.9 collective-permute-start.29
  311.3 7.2 %collective-permute-start.31 = (f32[2,20,2,128]{3,2,1,0:T(2,128)S(1)}, f32[2,20,2,128]{3,2,1,0:T(2,128)S(1)}, u32[]{:S(2)}, u32[]{:S(2)}) collective-permute-start(f32[2,20,2,128]{3,2,1,0:T(2,128)S(1)} %get-tuple-element.29), channel_id=1, source_target_pairs={{0,1},{1,2},{2,3},{3,4},{4,5},{5,6},{6,7},{8,9},{9,10},{10,11},{11... | collective-permute-start | bytes 122888 | tf_op jit(solution)/shard_map/ppermute | solution.py:21
  319.5 16.7 %copy.521 = f32[2,16,32,128]{0,3,2,1:T(8,128)} copy(f32[2,16,32,128]{3,2,1,0:T(8,128)S(1)} %fusion.22) | data formatting | bytes 1048576 | tf_op jit(solution)/shard_map/div | solution.py:86
  341.3 16.8 %copy.522 = f32[2,16,32,128]{0,3,2,1:T(8,128)} copy(f32[2,16,32,128]{3,2,1,0:T(8,128)S(1)} %fusion.10) | data formatting | bytes 1048576 | tf_op jit(solution)/shard_map/div | solution.py:86
  362.6 183.4 %psum.7 = f32[1,2,256,8]{2,3,1,0:T(8,128)} all-reduce(f32[1,2,256,8]{2,3,1,0:T(8,128)S(1)} %bitcast.70), channel_id=1, replica_groups=mesh['shot'=4,'gx'=4,'gy'=8] {'gx','gy'}, use_global_device_ids=true, to_apply=%region_1.2 | all-reduce | flops 4096 | bytes 32768 | tf_op jit(solution)/shard_map/psum | solution.py:138
  (164 shorter events, 112.2 us)
Async XLA Ops:
  7.2 54.9 %all-gather.2.cloned.1.call-start = ((), (), s32[]{:S(2)}) async-start(), calls=%async_computation | async-start | bytes 4456448 | tf_op jit(solution)/shard_map/all_gather | solution.py:113
  8.8 17.0 %collective-permute-start = (f32[2,2,32,128]{3,2,1,0:T(8,128)S(1)}, f32[2,2,32,128]{3,2,1,0:T(8,128)S(1)}, u32[]{:S(2)}, u32[]{:S(2)}) collective-permute-start(f32[2,2,32,128]{3,2,1,0:T(8,128)S(1)} %get-tuple-element.104), channel_id=1, source_target_pairs={{8,0},{16,8},{24,16},{9,1},{17,9},{25,17},{10,2},{18,10},{26,18},{... | collective-permute-start | bytes 196616 | tf_op jit(solution)/shard_map/ppermute | solution.py:23
  10.1 15.8 %collective-permute-start.1 = (f32[2,2,32,128]{3,2,1,0:T(8,128)S(1)}, f32[2,2,32,128]{3,2,1,0:T(8,128)S(1)}, u32[]{:S(2)}, u32[]{:S(2)}) collective-permute-start(f32[2,2,32,128]{3,2,1,0:T(8,128)S(1)} %get-tuple-element.105), channel_id=1, source_target_pairs={{0,8},{8,16},{16,24},{1,9},{9,17},{17,25},{2,10},{10,18},{18,26},{... | collective-permute-start | bytes 196616 | tf_op jit(solution)/shard_map/ppermute | solution.py:21
  26.9 7.7 %collective-permute-start.2 = (f32[2,20,2,128]{3,2,1,0:T(2,128)S(1)}, f32[2,20,2,128]{3,2,1,0:T(2,128)S(1)}, u32[]{:S(2)}, u32[]{:S(2)}) collective-permute-start(f32[2,20,2,128]{3,2,1,0:T(2,128)S(1)} %get-tuple-element.56), channel_id=1, source_target_pairs={{1,0},{2,1},{3,2},{4,3},{5,4},{6,5},{7,6},{9,8},{10,9},{11,10},{12... | collective-permute-start | bytes 122888 | tf_op jit(solution)/shard_map/ppermute | solution.py:23
  28.2 7.9 %collective-permute-start.3 = (f32[2,20,2,128]{3,2,1,0:T(2,128)S(1)}, f32[2,20,2,128]{3,2,1,0:T(2,128)S(1)}, u32[]{:S(2)}, u32[]{:S(2)}) collective-permute-start(f32[2,20,2,128]{3,2,1,0:T(2,128)S(1)} %get-tuple-element.57), channel_id=1, source_target_pairs={{0,1},{1,2},{2,3},{3,4},{4,5},{5,6},{6,7},{8,9},{9,10},{10,11},{11... | collective-permute-start | bytes 122888 | tf_op jit(solution)/shard_map/ppermute | solution.py:21
  68.1 6.8 %collective-permute-start.4 = (f32[2,2,32,128]{3,2,1,0:T(8,128)S(1)}, f32[2,2,32,128]{3,2,1,0:T(8,128)S(1)}, u32[]{:S(2)}, u32[]{:S(2)}) collective-permute-start(f32[2,2,32,128]{3,2,1,0:T(8,128)S(1)} %get-tuple-element.98), channel_id=1, source_target_pairs={{8,0},{16,8},{24,16},{9,1},{17,9},{25,17},{10,2},{18,10},{26,18},{... | collective-permute-start | bytes 196616 | tf_op jit(solution)/shard_map/ppermute | solution.py:23
  76.1 28.0 %collective-permute-start.6 = (f32[2,20,2,128]{3,2,1,0:T(2,128)S(1)}, f32[2,20,2,128]{3,2,1,0:T(2,128)S(1)}, u32[]{:S(2)}, u32[]{:S(2)}) collective-permute-start(f32[2,20,2,128]{3,2,1,0:T(2,128)S(1)} %get-tuple-element.52), channel_id=1, source_target_pairs={{1,0},{2,1},{3,2},{4,3},{5,4},{6,5},{7,6},{9,8},{10,9},{11,10},{12... | collective-permute-start | bytes 122888 | tf_op jit(solution)/shard_map/ppermute | solution.py:23
  77.4 26.7 %collective-permute-start.7 = (f32[2,20,2,128]{3,2,1,0:T(2,128)S(1)}, f32[2,20,2,128]{3,2,1,0:T(2,128)S(1)}, u32[]{:S(2)}, u32[]{:S(2)}) collective-permute-start(f32[2,20,2,128]{3,2,1,0:T(2,128)S(1)} %get-tuple-element.53), channel_id=1, source_target_pairs={{0,1},{1,2},{2,3},{3,4},{4,5},{5,6},{6,7},{8,9},{9,10},{10,11},{11... | collective-permute-start | bytes 122888 | tf_op jit(solution)/shard_map/ppermute | solution.py:21
  107.5 6.9 %collective-permute-start.9 = (f32[2,2,32,128]{3,2,1,0:T(8,128)S(1)}, f32[2,2,32,128]{3,2,1,0:T(8,128)S(1)}, u32[]{:S(2)}, u32[]{:S(2)}) collective-permute-start(f32[2,2,32,128]{3,2,1,0:T(8,128)S(1)} %get-tuple-element.93), channel_id=1, source_target_pairs={{0,8},{8,16},{16,24},{1,9},{9,17},{17,25},{2,10},{10,18},{18,26},{... | collective-permute-start | bytes 196616 | tf_op jit(solution)/shard_map/ppermute | solution.py:21
  114.5 28.5 %collective-permute-start.10 = (f32[2,20,2,128]{3,2,1,0:T(2,128)S(1)}, f32[2,20,2,128]{3,2,1,0:T(2,128)S(1)}, u32[]{:S(2)}, u32[]{:S(2)}) collective-permute-start(f32[2,20,2,128]{3,2,1,0:T(2,128)S(1)} %get-tuple-element.48), channel_id=1, source_target_pairs={{1,0},{2,1},{3,2},{4,3},{5,4},{6,5},{7,6},{9,8},{10,9},{11,10},{12... | collective-permute-start | bytes 122888 | tf_op jit(solution)/shard_map/ppermute | solution.py:23
  115.8 27.2 %collective-permute-start.11 = (f32[2,20,2,128]{3,2,1,0:T(2,128)S(1)}, f32[2,20,2,128]{3,2,1,0:T(2,128)S(1)}, u32[]{:S(2)}, u32[]{:S(2)}) collective-permute-start(f32[2,20,2,128]{3,2,1,0:T(2,128)S(1)} %get-tuple-element.49), channel_id=1, source_target_pairs={{0,1},{1,2},{2,3},{3,4},{4,5},{5,6},{6,7},{8,9},{9,10},{10,11},{11... | collective-permute-start | bytes 122888 | tf_op jit(solution)/shard_map/ppermute | solution.py:21
  146.4 6.8 %collective-permute-start.13 = (f32[2,2,32,128]{3,2,1,0:T(8,128)S(1)}, f32[2,2,32,128]{3,2,1,0:T(8,128)S(1)}, u32[]{:S(2)}, u32[]{:S(2)}) collective-permute-start(f32[2,2,32,128]{3,2,1,0:T(8,128)S(1)} %get-tuple-element.87), channel_id=1, source_target_pairs={{0,8},{8,16},{16,24},{1,9},{9,17},{17,25},{2,10},{10,18},{18,26},{... | collective-permute-start | bytes 196616 | tf_op jit(solution)/shard_map/ppermute | solution.py:21
  153.2 28.9 %collective-permute-start.14 = (f32[2,20,2,128]{3,2,1,0:T(2,128)S(1)}, f32[2,20,2,128]{3,2,1,0:T(2,128)S(1)}, u32[]{:S(2)}, u32[]{:S(2)}) collective-permute-start(f32[2,20,2,128]{3,2,1,0:T(2,128)S(1)} %get-tuple-element.44), channel_id=1, source_target_pairs={{1,0},{2,1},{3,2},{4,3},{5,4},{6,5},{7,6},{9,8},{10,9},{11,10},{12... | collective-permute-start | bytes 122888 | tf_op jit(solution)/shard_map/ppermute | solution.py:23
  154.5 27.6 %collective-permute-start.15 = (f32[2,20,2,128]{3,2,1,0:T(2,128)S(1)}, f32[2,20,2,128]{3,2,1,0:T(2,128)S(1)}, u32[]{:S(2)}, u32[]{:S(2)}) collective-permute-start(f32[2,20,2,128]{3,2,1,0:T(2,128)S(1)} %get-tuple-element.45), channel_id=1, source_target_pairs={{0,1},{1,2},{2,3},{3,4},{4,5},{5,6},{6,7},{8,9},{9,10},{10,11},{11... | collective-permute-start | bytes 122888 | tf_op jit(solution)/shard_map/ppermute | solution.py:21
  185.6 6.8 %collective-permute-start.17 = (f32[2,2,32,128]{3,2,1,0:T(8,128)S(1)}, f32[2,2,32,128]{3,2,1,0:T(8,128)S(1)}, u32[]{:S(2)}, u32[]{:S(2)}) collective-permute-start(f32[2,2,32,128]{3,2,1,0:T(8,128)S(1)} %get-tuple-element.81), channel_id=1, source_target_pairs={{0,8},{8,16},{16,24},{1,9},{9,17},{17,25},{2,10},{10,18},{18,26},{... | collective-permute-start | bytes 196616 | tf_op jit(solution)/shard_map/ppermute | solution.py:21
  192.4 29.1 %collective-permute-start.18 = (f32[2,20,2,128]{3,2,1,0:T(2,128)S(1)}, f32[2,20,2,128]{3,2,1,0:T(2,128)S(1)}, u32[]{:S(2)}, u32[]{:S(2)}) collective-permute-start(f32[2,20,2,128]{3,2,1,0:T(2,128)S(1)} %get-tuple-element.40), channel_id=1, source_target_pairs={{1,0},{2,1},{3,2},{4,3},{5,4},{6,5},{7,6},{9,8},{10,9},{11,10},{12... | collective-permute-start | bytes 122888 | tf_op jit(solution)/shard_map/ppermute | solution.py:23
  193.7 27.8 %collective-permute-start.19 = (f32[2,20,2,128]{3,2,1,0:T(2,128)S(1)}, f32[2,20,2,128]{3,2,1,0:T(2,128)S(1)}, u32[]{:S(2)}, u32[]{:S(2)}) collective-permute-start(f32[2,20,2,128]{3,2,1,0:T(2,128)S(1)} %get-tuple-element.41), channel_id=1, source_target_pairs={{0,1},{1,2},{2,3},{3,4},{4,5},{5,6},{6,7},{8,9},{9,10},{10,11},{11... | collective-permute-start | bytes 122888 | tf_op jit(solution)/shard_map/ppermute | solution.py:21
  231.7 28.9 %collective-permute-start.22 = (f32[2,20,2,128]{3,2,1,0:T(2,128)S(1)}, f32[2,20,2,128]{3,2,1,0:T(2,128)S(1)}, u32[]{:S(2)}, u32[]{:S(2)}) collective-permute-start(f32[2,20,2,128]{3,2,1,0:T(2,128)S(1)} %get-tuple-element.36), channel_id=1, source_target_pairs={{1,0},{2,1},{3,2},{4,3},{5,4},{6,5},{7,6},{9,8},{10,9},{11,10},{12... | collective-permute-start | bytes 122888 | tf_op jit(solution)/shard_map/ppermute | solution.py:23
  233.0 27.6 %collective-permute-start.23 = (f32[2,20,2,128]{3,2,1,0:T(2,128)S(1)}, f32[2,20,2,128]{3,2,1,0:T(2,128)S(1)}, u32[]{:S(2)}, u32[]{:S(2)}) collective-permute-start(f32[2,20,2,128]{3,2,1,0:T(2,128)S(1)} %get-tuple-element.37), channel_id=1, source_target_pairs={{0,1},{1,2},{2,3},{3,4},{4,5},{5,6},{6,7},{8,9},{9,10},{10,11},{11... | collective-permute-start | bytes 122888 | tf_op jit(solution)/shard_map/ppermute | solution.py:21
  264.1 6.8 %collective-permute-start.25 = (f32[2,2,32,128]{3,2,1,0:T(8,128)S(1)}, f32[2,2,32,128]{3,2,1,0:T(8,128)S(1)}, u32[]{:S(2)}, u32[]{:S(2)}) collective-permute-start(f32[2,2,32,128]{3,2,1,0:T(8,128)S(1)} %get-tuple-element.69), channel_id=1, source_target_pairs={{0,8},{8,16},{16,24},{1,9},{9,17},{17,25},{2,10},{10,18},{18,26},{... | collective-permute-start | bytes 196616 | tf_op jit(solution)/shard_map/ppermute | solution.py:21
  270.9 28.9 %collective-permute-start.26 = (f32[2,20,2,128]{3,2,1,0:T(2,128)S(1)}, f32[2,20,2,128]{3,2,1,0:T(2,128)S(1)}, u32[]{:S(2)}, u32[]{:S(2)}) collective-permute-start(f32[2,20,2,128]{3,2,1,0:T(2,128)S(1)} %get-tuple-element.32), channel_id=1, source_target_pairs={{1,0},{2,1},{3,2},{4,3},{5,4},{6,5},{7,6},{9,8},{10,9},{11,10},{12... | collective-permute-start | bytes 122888 | tf_op jit(solution)/shard_map/ppermute | solution.py:23
  272.2 27.6 %collective-permute-start.27 = (f32[2,20,2,128]{3,2,1,0:T(2,128)S(1)}, f32[2,20,2,128]{3,2,1,0:T(2,128)S(1)}, u32[]{:S(2)}, u32[]{:S(2)}) collective-permute-start(f32[2,20,2,128]{3,2,1,0:T(2,128)S(1)} %get-tuple-element.33), channel_id=1, source_target_pairs={{0,1},{1,2},{2,3},{3,4},{4,5},{5,6},{6,7},{8,9},{9,10},{10,11},{11... | collective-permute-start | bytes 122888 | tf_op jit(solution)/shard_map/ppermute | solution.py:21
  310.0 29.1 %collective-permute-start.30 = (f32[2,20,2,128]{3,2,1,0:T(2,128)S(1)}, f32[2,20,2,128]{3,2,1,0:T(2,128)S(1)}, u32[]{:S(2)}, u32[]{:S(2)}) collective-permute-start(f32[2,20,2,128]{3,2,1,0:T(2,128)S(1)} %get-tuple-element.28), channel_id=1, source_target_pairs={{1,0},{2,1},{3,2},{4,3},{5,4},{6,5},{7,6},{9,8},{10,9},{11,10},{12... | collective-permute-start | bytes 122888 | tf_op jit(solution)/shard_map/ppermute | solution.py:23
  311.3 27.8 %collective-permute-start.31 = (f32[2,20,2,128]{3,2,1,0:T(2,128)S(1)}, f32[2,20,2,128]{3,2,1,0:T(2,128)S(1)}, u32[]{:S(2)}, u32[]{:S(2)}) collective-permute-start(f32[2,20,2,128]{3,2,1,0:T(2,128)S(1)} %get-tuple-element.29), channel_id=1, source_target_pairs={{0,1},{1,2},{2,3},{3,4},{4,5},{5,6},{6,7},{8,9},{9,10},{10,11},{11... | collective-permute-start | bytes 122888 | tf_op jit(solution)/shard_map/ppermute | solution.py:21
  (22 other events, 717.0 us)
Sparse Core Ops, SparseCore 0:
  9.7 52.3 all-gather.1
where the time goes:
time: 554 us; the launch traced here: 553 us
  blocking collectives  183 us (33%)
  local copies, waits for them, and re-layouts  177 us (32%)
  starting transfers between devices  113 us (20%)
  waiting for transfers between devices  39.1 us (7%)
  other arithmetic  24.3 us (4%)
  between operations  16 us (3%)
    psum x1, blocking collectives, local(): traces = lax.psum(jnp.stack(recorded, axis=-1), ('gx', 'gy'))  183 us
    div x8, local copies, waits for them, and re-layouts, advance(): (2.0 * middle - (1.0 - damp) * previous + coef * laplace(extended) + inje...  134 us
    ppermute x16, starting transfers between devices, extended_2(): lax.ppermute(tail, axis, [(i, (i + 1) % count) for i in range(ends)])  92.2 us
    all_gather x1, waiting for transfers between devices, local(): piece = lax.all_gather(model_tiles, ('shot', 'gx'), axis=0, tiled=True)  24.6 us
    gather x8, local copies, waits for them, and re-layouts, sample(): field[:, jnp.clip(local_x, 0, size_x - 1), jnp.clip(local_y, 0, size_y -...  23.6 us
    ppermute x16, starting transfers between devices, extended_2(): lax.ppermute(head, axis, [((i + 1) % count, i) for i in range(ends)])  20.7 us
    div x8, other arithmetic, advance(): (2.0 * middle - (1.0 - damp) * previous + coef * laplace(extended) + inje...  16.9 us
    slice x16, local copies, waits for them, and re-layouts, depth_ahead(): return jnp.concatenate([field[..., reach:], filler], axis=-1)  12.5 us
  transfers between devices with their start and end apart: 33, of which 17 were waited for; matrix products, arithmetic and copies ran while one was open for 29% of the time, Pallas kernels for 0%

commit v1 on v0

--- a/solution.py
+++ b/solution.py
@@ -135,7 +135,9 @@
         recorded.append(sample(fresh, receiver_cells, x_start, y_start))
         previous = current
         current = fresh
-    traces = lax.psum(jnp.stack(recorded, axis=-1), ("gx", "gy"))
+    local_block = jnp.stack(recorded, axis=-1)
+    everything = lax.psum(local_block, "gy")
+    traces = lax.psum(everything, "gx")
     return (current[None], previous[None], traces[None])
 
 

time: 554 us -> 432 us (0.78)
  blocking collectives: 183 us -> 60.9 us
    psum x1 -> x2, blocking collectives: 183 us -> 60.9 us  [the longest x1 41.2 us: local(): everything = lax.psum(local_block, 'gy')]
  transfers between devices with their start and end apart: 33 -> 33, of which waited for: 17 -> 17; matrix products, arithmetic and copies ran while one was open for 29% -> 37% of each run, Pallas kernels for 0% -> 0%
where the time goes in v1:
time: 432 us; the launch traced here: 430 us
  local copies, waits for them, and re-layouts  177 us (41%)
  starting transfers between devices  113 us (26%)
  blocking collectives  60.9 us (14%)
  waiting for transfers between devices  39.1 us (9%)
  other arithmetic  24.3 us (6%)
  between operations  16 us (4%)
    div x8, local copies, waits for them, and re-layouts, advance(): (2.0 * middle - (1.0 - damp) * previous + coef * laplace(extended) + inje...  133 us
    ppermute x16, starting transfers between devices, extended_2(): lax.ppermute(tail, axis, [(i, (i + 1) % count) for i in range(ends)])  92.4 us
    psum x1, blocking collectives, local(): everything = lax.psum(local_block, 'gy')  41.2 us
    all_gather x1, waiting for transfers between devices, local(): piece = lax.all_gather(model_tiles, ('shot', 'gx'), axis=0, tiled=True)  24.6 us
    gather x8, local copies, waits for them, and re-layouts, sample(): field[:, jnp.clip(local_x, 0, size_x - 1), jnp.clip(local_y, 0, size_y -...  23.6 us
    ppermute x16, starting transfers between devices, extended_2(): lax.ppermute(head, axis, [((i + 1) % count, i) for i in range(ends)])  20.7 us
    psum x1, blocking collectives, local(): traces = lax.psum(everything, 'gx')  19.7 us
    div x8, other arithmetic, advance(): (2.0 * middle - (1.0 - damp) * previous + coef * laplace(extended) + inje...  16.9 us
  transfers between devices with their start and end apart: 33, of which 17 were waited for; matrix products, arithmetic and copies ran while one was open for 37% of the time, Pallas kernels for 0%

profile of v1, /device:TPU:0, one launch (start us, length us, event | category | flops | bytes accessed | tf_op | source)
XLA Modules:
  0.0 430.3 jit_solution(1766614489517195570)
XLA Ops:
  28.2 6.1 %collective-permute-start.3 = (f32[2,20,2,128]{3,2,1,0:T(2,128)S(1)}, f32[2,20,2,128]{3,2,1,0:T(2,128)S(1)}, u32[]{:S(2)}, u32[]{:S(2)}) collective-permute-start(f32[2,20,2,128]{3,2,1,0:T(2,128)S(1)} %get-tuple-element.57), channel_id=1, source_target_pairs={{0,1},{1,2},{2,3},{3,4},{4,5},{5,6},{6,7},{8,9},{9,10},{10,11},{11... | collective-permute-start | bytes 122888 | tf_op jit(solution)/shard_map/ppermute | solution.py:21
  37.5 24.6 %all-gather.2.cloned.1.call-done = f32[256,32,128]{2,1,0:T(8,128)} async-done(((f32[16,32,128]{2,1,0:T(8,128)}), f32[256,32,128]{2,1,0:T(8,128)}) %all-gather.2.cloned.1.call-update) | async-done | bytes 4194320 | tf_op jit(solution)/shard_map/all_gather | solution.py:113
  77.4 6.1 %collective-permute-start.7 = (f32[2,20,2,128]{3,2,1,0:T(2,128)S(1)}, f32[2,20,2,128]{3,2,1,0:T(2,128)S(1)}, u32[]{:S(2)}, u32[]{:S(2)}) collective-permute-start(f32[2,20,2,128]{3,2,1,0:T(2,128)S(1)} %get-tuple-element.53), channel_id=1, source_target_pairs={{0,1},{1,2},{2,3},{3,4},{4,5},{5,6},{6,7},{8,9},{9,10},{10,11},{11... | collective-permute-start | bytes 122888 | tf_op jit(solution)/shard_map/ppermute | solution.py:21
  84.4 16.6 %copy.515 = f32[2,16,32,128]{0,3,2,1:T(8,128)} copy(f32[2,16,32,128]{3,2,1,0:T(8,128)S(1)} %fusion.94) | data formatting | bytes 1048576 | tf_op jit(solution)/shard_map/div | solution.py:86
  107.5 5.0 %collective-permute-start.9 = (f32[2,2,32,128]{3,2,1,0:T(8,128)S(1)}, f32[2,2,32,128]{3,2,1,0:T(8,128)S(1)}, u32[]{:S(2)}, u32[]{:S(2)}) collective-permute-start(f32[2,2,32,128]{3,2,1,0:T(8,128)S(1)} %get-tuple-element.93), channel_id=1, source_target_pairs={{0,8},{8,16},{16,24},{1,9},{9,17},{17,25},{2,10},{10,18},{18,26},{... | collective-permute-start | bytes 196616 | tf_op jit(solution)/shard_map/ppermute | solution.py:21
  115.8 6.5 %collective-permute-start.11 = (f32[2,20,2,128]{3,2,1,0:T(2,128)S(1)}, f32[2,20,2,128]{3,2,1,0:T(2,128)S(1)}, u32[]{:S(2)}, u32[]{:S(2)}) collective-permute-start(f32[2,20,2,128]{3,2,1,0:T(2,128)S(1)} %get-tuple-element.49), channel_id=1, source_target_pairs={{0,1},{1,2},{2,3},{3,4},{4,5},{5,6},{6,7},{8,9},{9,10},{10,11},{11... | collective-permute-start | bytes 122888 | tf_op jit(solution)/shard_map/ppermute | solution.py:21
  123.3 16.6 %copy.516 = f32[2,16,32,128]{0,3,2,1:T(8,128)} copy(f32[2,16,32,128]{3,2,1,0:T(8,128)S(1)} %fusion.82) | data formatting | bytes 1048576 | tf_op jit(solution)/shard_map/div | solution.py:86
  146.4 4.9 %collective-permute-start.13 = (f32[2,2,32,128]{3,2,1,0:T(8,128)S(1)}, f32[2,2,32,128]{3,2,1,0:T(8,128)S(1)}, u32[]{:S(2)}, u32[]{:S(2)}) collective-permute-start(f32[2,2,32,128]{3,2,1,0:T(8,128)S(1)} %get-tuple-element.87), channel_id=1, source_target_pairs={{0,8},{8,16},{16,24},{1,9},{9,17},{17,25},{2,10},{10,18},{18,26},{... | collective-permute-start | bytes 196616 | tf_op jit(solution)/shard_map/ppermute | solution.py:21
  154.5 7.0 %collective-permute-start.15 = (f32[2,20,2,128]{3,2,1,0:T(2,128)S(1)}, f32[2,20,2,128]{3,2,1,0:T(2,128)S(1)}, u32[]{:S(2)}, u32[]{:S(2)}) collective-permute-start(f32[2,20,2,128]{3,2,1,0:T(2,128)S(1)} %get-tuple-element.45), channel_id=1, source_target_pairs={{0,1},{1,2},{2,3},{3,4},{4,5},{5,6},{6,7},{8,9},{9,10},{10,11},{11... | collective-permute-start | bytes 122888 | tf_op jit(solution)/shard_map/ppermute | solution.py:21
  162.4 16.6 %copy.517 = f32[2,16,32,128]{0,3,2,1:T(8,128)} copy(f32[2,16,32,128]{3,2,1,0:T(8,128)S(1)} %fusion.70) | data formatting | bytes 1048576 | tf_op jit(solution)/shard_map/div | solution.py:86
  185.6 4.9 %collective-permute-start.17 = (f32[2,2,32,128]{3,2,1,0:T(8,128)S(1)}, f32[2,2,32,128]{3,2,1,0:T(8,128)S(1)}, u32[]{:S(2)}, u32[]{:S(2)}) collective-permute-start(f32[2,2,32,128]{3,2,1,0:T(8,128)S(1)} %get-tuple-element.81), channel_id=1, source_target_pairs={{0,8},{8,16},{16,24},{1,9},{9,17},{17,25},{2,10},{10,18},{18,26},{... | collective-permute-start | bytes 196616 | tf_op jit(solution)/shard_map/ppermute | solution.py:21
  193.7 7.1 %collective-permute-start.19 = (f32[2,20,2,128]{3,2,1,0:T(2,128)S(1)}, f32[2,20,2,128]{3,2,1,0:T(2,128)S(1)}, u32[]{:S(2)}, u32[]{:S(2)}) collective-permute-start(f32[2,20,2,128]{3,2,1,0:T(2,128)S(1)} %get-tuple-element.41), channel_id=1, source_target_pairs={{0,1},{1,2},{2,3},{3,4},{4,5},{5,6},{6,7},{8,9},{9,10},{10,11},{11... | collective-permute-start | bytes 122888 | tf_op jit(solution)/shard_map/ppermute | solution.py:21
  201.8 16.6 %copy.518 = f32[2,16,32,128]{0,3,2,1:T(8,128)} copy(f32[2,16,32,128]{3,2,1,0:T(8,128)S(1)} %fusion.58) | data formatting | bytes 1048576 | tf_op jit(solution)/shard_map/div | solution.py:86
  224.9 4.9 %collective-permute-start.21 = (f32[2,2,32,128]{3,2,1,0:T(8,128)S(1)}, f32[2,2,32,128]{3,2,1,0:T(8,128)S(1)}, u32[]{:S(2)}, u32[]{:S(2)}) collective-permute-start(f32[2,2,32,128]{3,2,1,0:T(8,128)S(1)} %get-tuple-element.75), channel_id=1, source_target_pairs={{0,8},{8,16},{16,24},{1,9},{9,17},{17,25},{2,10},{10,18},{18,26},{... | collective-permute-start | bytes 196616 | tf_op jit(solution)/shard_map/ppermute | solution.py:21
  233.0 7.0 %collective-permute-start.23 = (f32[2,20,2,128]{3,2,1,0:T(2,128)S(1)}, f32[2,20,2,128]{3,2,1,0:T(2,128)S(1)}, u32[]{:S(2)}, u32[]{:S(2)}) collective-permute-start(f32[2,20,2,128]{3,2,1,0:T(2,128)S(1)} %get-tuple-element.37), channel_id=1, source_target_pairs={{0,1},{1,2},{2,3},{3,4},{4,5},{5,6},{6,7},{8,9},{9,10},{10,11},{11... | collective-permute-start | bytes 122888 | tf_op jit(solution)/shard_map/ppermute | solution.py:21
  240.9 16.6 %copy.519 = f32[2,16,32,128]{0,3,2,1:T(8,128)} copy(f32[2,16,32,128]{3,2,1,0:T(8,128)S(1)} %fusion.46) | data formatting | bytes 1048576 | tf_op jit(solution)/shard_map/div | solution.py:86
  264.1 4.9 %collective-permute-start.25 = (f32[2,2,32,128]{3,2,1,0:T(8,128)S(1)}, f32[2,2,32,128]{3,2,1,0:T(8,128)S(1)}, u32[]{:S(2)}, u32[]{:S(2)}) collective-permute-start(f32[2,2,32,128]{3,2,1,0:T(8,128)S(1)} %get-tuple-element.69), channel_id=1, source_target_pairs={{0,8},{8,16},{16,24},{1,9},{9,17},{17,25},{2,10},{10,18},{18,26},{... | collective-permute-start | bytes 196616 | tf_op jit(solution)/shard_map/ppermute | solution.py:21
  272.2 7.0 %collective-permute-start.27 = (f32[2,20,2,128]{3,2,1,0:T(2,128)S(1)}, f32[2,20,2,128]{3,2,1,0:T(2,128)S(1)}, u32[]{:S(2)}, u32[]{:S(2)}) collective-permute-start(f32[2,20,2,128]{3,2,1,0:T(2,128)S(1)} %get-tuple-element.33), channel_id=1, source_target_pairs={{0,1},{1,2},{2,3},{3,4},{4,5},{5,6},{6,7},{8,9},{9,10},{10,11},{11... | collective-permute-start | bytes 122888 | tf_op jit(solution)/shard_map/ppermute | solution.py:21
  280.1 16.6 %copy.520 = f32[2,16,32,128]{0,3,2,1:T(8,128)} copy(f32[2,16,32,128]{3,2,1,0:T(8,128)S(1)} %fusion.34) | data formatting | bytes 1048576 | tf_op jit(solution)/shard_map/div | solution.py:86
  311.4 7.2 %collective-permute-start.31 = (f32[2,20,2,128]{3,2,1,0:T(2,128)S(1)}, f32[2,20,2,128]{3,2,1,0:T(2,128)S(1)}, u32[]{:S(2)}, u32[]{:S(2)}) collective-permute-start(f32[2,20,2,128]{3,2,1,0:T(2,128)S(1)} %get-tuple-element.29), channel_id=1, source_target_pairs={{0,1},{1,2},{2,3},{3,4},{4,5},{5,6},{6,7},{8,9},{9,10},{10,11},{11... | collective-permute-start | bytes 122888 | tf_op jit(solution)/shard_map/ppermute | solution.py:21
  319.5 16.6 %copy.521 = f32[2,16,32,128]{0,3,2,1:T(8,128)} copy(f32[2,16,32,128]{3,2,1,0:T(8,128)S(1)} %fusion.22) | data formatting | bytes 1048576 | tf_op jit(solution)/shard_map/div | solution.py:86
  341.4 16.7 %copy.522 = f32[2,16,32,128]{0,3,2,1:T(8,128)} copy(f32[2,16,32,128]{3,2,1,0:T(8,128)S(1)} %fusion.10) | data formatting | bytes 1048576 | tf_op jit(solution)/shard_map/div | solution.py:86
  362.6 41.2 %psum.14 = f32[2,256,8]{1,2,0:T(8,128)S(1)} all-reduce(f32[2,256,8]{1,2,0:T(8,128)S(1)} %stack.2), channel_id=1, replica_groups=mesh['shot'=4,'gx'=4,'gy'=8] {'gy'}, use_global_device_ids=true, to_apply=%region_1.2 | all-reduce | flops 4096 | bytes 32768 | tf_op jit(solution)/shard_map/psum | solution.py:139
  403.8 19.7 %psum.15 = f32[1,2,256,8]{2,3,1,0:T(8,128)} all-reduce(f32[1,2,256,8]{2,3,1,0:T(8,128)S(1)} %bitcast.70), channel_id=1, replica_groups=mesh['shot'=4,'gx'=4,'gy'=8] {'gx'}, use_global_device_ids=true, to_apply=%region_2.3 | all-reduce | flops 4096 | bytes 32768 | tf_op jit(solution)/shard_map/psum | solution.py:140
  (165 shorter events, 117.2 us)
Async XLA Ops:
  7.2 54.9 %all-gather.2.cloned.1.call-start = ((), (), s32[]{:S(2)}) async-start(), calls=%async_computation | async-start | bytes 4456448 | tf_op jit(solution)/shard_map/all_gather | solution.py:113
  8.8 17.0 %collective-permute-start = (f32[2,2,32,128]{3,2,1,0:T(8,128)S(1)}, f32[2,2,32,128]{3,2,1,0:T(8,128)S(1)}, u32[]{:S(2)}, u32[]{:S(2)}) collective-permute-start(f32[2,2,32,128]{3,2,1,0:T(8,128)S(1)} %get-tuple-element.104), channel_id=1, source_target_pairs={{8,0},{16,8},{24,16},{9,1},{17,9},{25,17},{10,2},{18,10},{26,18},{... | collective-permute-start | bytes 196616 | tf_op jit(solution)/shard_map/ppermute | solution.py:23
  10.1 15.8 %collective-permute-start.1 = (f32[2,2,32,128]{3,2,1,0:T(8,128)S(1)}, f32[2,2,32,128]{3,2,1,0:T(8,128)S(1)}, u32[]{:S(2)}, u32[]{:S(2)}) collective-permute-start(f32[2,2,32,128]{3,2,1,0:T(8,128)S(1)} %get-tuple-element.105), channel_id=1, source_target_pairs={{0,8},{8,16},{16,24},{1,9},{9,17},{17,25},{2,10},{10,18},{18,26},{... | collective-permute-start | bytes 196616 | tf_op jit(solution)/shard_map/ppermute | solution.py:21
  26.9 7.7 %collective-permute-start.2 = (f32[2,20,2,128]{3,2,1,0:T(2,128)S(1)}, f32[2,20,2,128]{3,2,1,0:T(2,128)S(1)}, u32[]{:S(2)}, u32[]{:S(2)}) collective-permute-start(f32[2,20,2,128]{3,2,1,0:T(2,128)S(1)} %get-tuple-element.56), channel_id=1, source_target_pairs={{1,0},{2,1},{3,2},{4,3},{5,4},{6,5},{7,6},{9,8},{10,9},{11,10},{12... | collective-permute-start | bytes 122888 | tf_op jit(solution)/shard_map/ppermute | solution.py:23
  28.2 7.9 %collective-permute-start.3 = (f32[2,20,2,128]{3,2,1,0:T(2,128)S(1)}, f32[2,20,2,128]{3,2,1,0:T(2,128)S(1)}, u32[]{:S(2)}, u32[]{:S(2)}) collective-permute-start(f32[2,20,2,128]{3,2,1,0:T(2,128)S(1)} %get-tuple-element.57), channel_id=1, source_target_pairs={{0,1},{1,2},{2,3},{3,4},{4,5},{5,6},{6,7},{8,9},{9,10},{10,11},{11... | collective-permute-start | bytes 122888 | tf_op jit(solution)/shard_map/ppermute | solution.py:21
  76.1 28.0 %collective-permute-start.6 = (f32[2,20,2,128]{3,2,1,0:T(2,128)S(1)}, f32[2,20,2,128]{3,2,1,0:T(2,128)S(1)}, u32[]{:S(2)}, u32[]{:S(2)}) collective-permute-start(f32[2,20,2,128]{3,2,1,0:T(2,128)S(1)} %get-tuple-element.52), channel_id=1, source_target_pairs={{1,0},{2,1},{3,2},{4,3},{5,4},{6,5},{7,6},{9,8},{10,9},{11,10},{12... | collective-permute-start | bytes 122888 | tf_op jit(solution)/shard_map/ppermute | solution.py:23
  77.4 26.7 %collective-permute-start.7 = (f32[2,20,2,128]{3,2,1,0:T(2,128)S(1)}, f32[2,20,2,128]{3,2,1,0:T(2,128)S(1)}, u32[]{:S(2)}, u32[]{:S(2)}) collective-permute-start(f32[2,20,2,128]{3,2,1,0:T(2,128)S(1)} %get-tuple-element.53), channel_id=1, source_target_pairs={{0,1},{1,2},{2,3},{3,4},{4,5},{5,6},{6,7},{8,9},{9,10},{10,11},{11... | collective-permute-start | bytes 122888 | tf_op jit(solution)/shard_map/ppermute | solution.py:21
  107.5 6.9 %collective-permute-start.9 = (f32[2,2,32,128]{3,2,1,0:T(8,128)S(1)}, f32[2,2,32,128]{3,2,1,0:T(8,128)S(1)}, u32[]{:S(2)}, u32[]{:S(2)}) collective-permute-start(f32[2,2,32,128]{3,2,1,0:T(8,128)S(1)} %get-tuple-element.93), channel_id=1, source_target_pairs={{0,8},{8,16},{16,24},{1,9},{9,17},{17,25},{2,10},{10,18},{18,26},{... | collective-permute-start | bytes 196616 | tf_op jit(solution)/shard_map/ppermute | solution.py:21
  114.5 28.4 %collective-permute-start.10 = (f32[2,20,2,128]{3,2,1,0:T(2,128)S(1)}, f32[2,20,2,128]{3,2,1,0:T(2,128)S(1)}, u32[]{:S(2)}, u32[]{:S(2)}) collective-permute-start(f32[2,20,2,128]{3,2,1,0:T(2,128)S(1)} %get-tuple-element.48), channel_id=1, source_target_pairs={{1,0},{2,1},{3,2},{4,3},{5,4},{6,5},{7,6},{9,8},{10,9},{11,10},{12... | collective-permute-start | bytes 122888 | tf_op jit(solution)/shard_map/ppermute | solution.py:23
  115.8 27.1 %collective-permute-start.11 = (f32[2,20,2,128]{3,2,1,0:T(2,128)S(1)}, f32[2,20,2,128]{3,2,1,0:T(2,128)S(1)}, u32[]{:S(2)}, u32[]{:S(2)}) collective-permute-start(f32[2,20,2,128]{3,2,1,0:T(2,128)S(1)} %get-tuple-element.49), channel_id=1, source_target_pairs={{0,1},{1,2},{2,3},{3,4},{4,5},{5,6},{6,7},{8,9},{9,10},{10,11},{11... | collective-permute-start | bytes 122888 | tf_op jit(solution)/shard_map/ppermute | solution.py:21
  153.2 28.9 %collective-permute-start.14 = (f32[2,20,2,128]{3,2,1,0:T(2,128)S(1)}, f32[2,20,2,128]{3,2,1,0:T(2,128)S(1)}, u32[]{:S(2)}, u32[]{:S(2)}) collective-permute-start(f32[2,20,2,128]{3,2,1,0:T(2,128)S(1)} %get-tuple-element.44), channel_id=1, source_target_pairs={{1,0},{2,1},{3,2},{4,3},{5,4},{6,5},{7,6},{9,8},{10,9},{11,10},{12... | collective-permute-start | bytes 122888 | tf_op jit(solution)/shard_map/ppermute | solution.py:23
  154.5 27.6 %collective-permute-start.15 = (f32[2,20,2,128]{3,2,1,0:T(2,128)S(1)}, f32[2,20,2,128]{3,2,1,0:T(2,128)S(1)}, u32[]{:S(2)}, u32[]{:S(2)}) collective-permute-start(f32[2,20,2,128]{3,2,1,0:T(2,128)S(1)} %get-tuple-element.45), channel_id=1, source_target_pairs={{0,1},{1,2},{2,3},{3,4},{4,5},{5,6},{6,7},{8,9},{9,10},{10,11},{11... | collective-permute-start | bytes 122888 | tf_op jit(solution)/shard_map/ppermute | solution.py:21
  185.6 6.8 %collective-permute-start.17 = (f32[2,2,32,128]{3,2,1,0:T(8,128)S(1)}, f32[2,2,32,128]{3,2,1,0:T(8,128)S(1)}, u32[]{:S(2)}, u32[]{:S(2)}) collective-permute-start(f32[2,2,32,128]{3,2,1,0:T(8,128)S(1)} %get-tuple-element.81), channel_id=1, source_target_pairs={{0,8},{8,16},{16,24},{1,9},{9,17},{17,25},{2,10},{10,18},{18,26},{... | collective-permute-start | bytes 196616 | tf_op jit(solution)/shard_map/ppermute | solution.py:21
  192.4 29.1 %collective-permute-start.18 = (f32[2,20,2,128]{3,2,1,0:T(2,128)S(1)}, f32[2,20,2,128]{3,2,1,0:T(2,128)S(1)}, u32[]{:S(2)}, u32[]{:S(2)}) collective-permute-start(f32[2,20,2,128]{3,2,1,0:T(2,128)S(1)} %get-tuple-element.40), channel_id=1, source_target_pairs={{1,0},{2,1},{3,2},{4,3},{5,4},{6,5},{7,6},{9,8},{10,9},{11,10},{12... | collective-permute-start | bytes 122888 | tf_op jit(solution)/shard_map/ppermute | solution.py:23
  193.7 27.8 %collective-permute-start.19 = (f32[2,20,2,128]{3,2,1,0:T(2,128)S(1)}, f32[2,20,2,128]{3,2,1,0:T(2,128)S(1)}, u32[]{:S(2)}, u32[]{:S(2)}) collective-permute-start(f32[2,20,2,128]{3,2,1,0:T(2,128)S(1)} %get-tuple-element.41), channel_id=1, source_target_pairs={{0,1},{1,2},{2,3},{3,4},{4,5},{5,6},{6,7},{8,9},{9,10},{10,11},{11... | collective-permute-start | bytes 122888 | tf_op jit(solution)/shard_map/ppermute | solution.py:21
  224.9 6.8 %collective-permute-start.21 = (f32[2,2,32,128]{3,2,1,0:T(8,128)S(1)}, f32[2,2,32,128]{3,2,1,0:T(8,128)S(1)}, u32[]{:S(2)}, u32[]{:S(2)}) collective-permute-start(f32[2,2,32,128]{3,2,1,0:T(8,128)S(1)} %get-tuple-element.75), channel_id=1, source_target_pairs={{0,8},{8,16},{16,24},{1,9},{9,17},{17,25},{2,10},{10,18},{18,26},{... | collective-permute-start | bytes 196616 | tf_op jit(solution)/shard_map/ppermute | solution.py:21
  231.7 28.9 %collective-permute-start.22 = (f32[2,20,2,128]{3,2,1,0:T(2,128)S(1)}, f32[2,20,2,128]{3,2,1,0:T(2,128)S(1)}, u32[]{:S(2)}, u32[]{:S(2)}) collective-permute-start(f32[2,20,2,128]{3,2,1,0:T(2,128)S(1)} %get-tuple-element.36), channel_id=1, source_target_pairs={{1,0},{2,1},{3,2},{4,3},{5,4},{6,5},{7,6},{9,8},{10,9},{11,10},{12... | collective-permute-start | bytes 122888 | tf_op jit(solution)/shard_map/ppermute | solution.py:23
  233.0 27.6 %collective-permute-start.23 = (f32[2,20,2,128]{3,2,1,0:T(2,128)S(1)}, f32[2,20,2,128]{3,2,1,0:T(2,128)S(1)}, u32[]{:S(2)}, u32[]{:S(2)}) collective-permute-start(f32[2,20,2,128]{3,2,1,0:T(2,128)S(1)} %get-tuple-element.37), channel_id=1, source_target_pairs={{0,1},{1,2},{2,3},{3,4},{4,5},{5,6},{6,7},{8,9},{9,10},{10,11},{11... | collective-permute-start | bytes 122888 | tf_op jit(solution)/shard_map/ppermute | solution.py:21
  264.1 6.8 %collective-permute-start.25 = (f32[2,2,32,128]{3,2,1,0:T(8,128)S(1)}, f32[2,2,32,128]{3,2,1,0:T(8,128)S(1)}, u32[]{:S(2)}, u32[]{:S(2)}) collective-permute-start(f32[2,2,32,128]{3,2,1,0:T(8,128)S(1)} %get-tuple-element.69), channel_id=1, source_target_pairs={{0,8},{8,16},{16,24},{1,9},{9,17},{17,25},{2,10},{10,18},{18,26},{... | collective-permute-start | bytes 196616 | tf_op jit(solution)/shard_map/ppermute | solution.py:21
  270.9 28.9 %collective-permute-start.26 = (f32[2,20,2,128]{3,2,1,0:T(2,128)S(1)}, f32[2,20,2,128]{3,2,1,0:T(2,128)S(1)}, u32[]{:S(2)}, u32[]{:S(2)}) collective-permute-start(f32[2,20,2,128]{3,2,1,0:T(2,128)S(1)} %get-tuple-element.32), channel_id=1, source_target_pairs={{1,0},{2,1},{3,2},{4,3},{5,4},{6,5},{7,6},{9,8},{10,9},{11,10},{12... | collective-permute-start | bytes 122888 | tf_op jit(solution)/shard_map/ppermute | solution.py:23
  272.2 27.6 %collective-permute-start.27 = (f32[2,20,2,128]{3,2,1,0:T(2,128)S(1)}, f32[2,20,2,128]{3,2,1,0:T(2,128)S(1)}, u32[]{:S(2)}, u32[]{:S(2)}) collective-permute-start(f32[2,20,2,128]{3,2,1,0:T(2,128)S(1)} %get-tuple-element.33), channel_id=1, source_target_pairs={{0,1},{1,2},{2,3},{3,4},{4,5},{5,6},{6,7},{8,9},{9,10},{10,11},{11... | collective-permute-start | bytes 122888 | tf_op jit(solution)/shard_map/ppermute | solution.py:21
  303.3 6.8 %collective-permute-start.29 = (f32[2,2,32,128]{3,2,1,0:T(8,128)S(1)}, f32[2,2,32,128]{3,2,1,0:T(8,128)S(1)}, u32[]{:S(2)}, u32[]{:S(2)}) collective-permute-start(f32[2,2,32,128]{3,2,1,0:T(8,128)S(1)} %get-tuple-element.63), channel_id=1, source_target_pairs={{0,8},{8,16},{16,24},{1,9},{9,17},{17,25},{2,10},{10,18},{18,26},{... | collective-permute-start | bytes 196616 | tf_op jit(solution)/shard_map/ppermute | solution.py:21
  310.1 29.1 %collective-permute-start.30 = (f32[2,20,2,128]{3,2,1,0:T(2,128)S(1)}, f32[2,20,2,128]{3,2,1,0:T(2,128)S(1)}, u32[]{:S(2)}, u32[]{:S(2)}) collective-permute-start(f32[2,20,2,128]{3,2,1,0:T(2,128)S(1)} %get-tuple-element.28), channel_id=1, source_target_pairs={{1,0},{2,1},{3,2},{4,3},{5,4},{6,5},{7,6},{9,8},{10,9},{11,10},{12... | collective-permute-start | bytes 122888 | tf_op jit(solution)/shard_map/ppermute | solution.py:23
  311.4 27.8 %collective-permute-start.31 = (f32[2,20,2,128]{3,2,1,0:T(2,128)S(1)}, f32[2,20,2,128]{3,2,1,0:T(2,128)S(1)}, u32[]{:S(2)}, u32[]{:S(2)}) collective-permute-start(f32[2,20,2,128]{3,2,1,0:T(2,128)S(1)} %get-tuple-element.29), channel_id=1, source_target_pairs={{0,1},{1,2},{2,3},{3,4},{4,5},{5,6},{6,7},{8,9},{9,10},{10,11},{11... | collective-permute-start | bytes 122888 | tf_op jit(solution)/shard_map/ppermute | solution.py:21
  (22 other events, 594.3 us)
Sparse Core Ops, SparseCore 0:
  9.7 52.3 all-gather.1
